TPU v7x, 128 devices: a whole 4x4x4 slice. The times are simulated.
128 devices in a mesh: rows: 32 (over x, y, z_lo), feat: 4 (over z_hi, core).
Axes of the slice: x: 4, y: 4, z: 4 (z_hi: 2, z_lo: 2; z = z_hi * 2 + z_lo), core: 2. Of those that a mesh axis runs over, the one named last changes fastest.
Arguments:
- node_feats: bfloat16 [256, 131072], P('feat', 'rows'), may hold values from -6 to 6
- tile_vals: bfloat16 [1024, 16, 128, 128], P('rows'), may hold values from -0.125 to 0.125
- tile_cols: int32 [1024, 16], P('rows'), may hold values from 0 to 1023, as said below
- weight: bfloat16 [256, 256], P(None, 'feat'), may hold values from -0.375 to 0.375
- bias_vec: float32 [256], P('feat'), may hold values from -3 to 3
- grad_out: bfloat16 [256, 131072], P('feat', 'rows'), may hold values from -6 to 6
Outputs:
- activated: bfloat16 [256, 131072], P('feat', 'rows')
- grad_feats: float32 [256, 131072], P('feat', 'rows')
- grad_weight: float32 [256, 256], P(None, 'feat')
- grad_bias: float32 [256], P('feat')
Inputs may be any that keep to these rules, and one draw needn't show every extreme that they name: `tile_cols`: among the tiles of one device's 32 blocks of rows, the column blocks held by any one owner (blocks o * 32 to o * 32 + 31) are at most 16 distinct ones and at least one; on every device some owner reaches 16.
All inputs are finite; a program needn't handle non-finite values.
Results may differ from a plain program's by a relative error of at most 0.007.
Values may be sent and summed in bfloat16 or wider, within the bound.
No kernel may reach another device: no remote copies, remote signals or barrier semaphores. Data moves between devices by JAX's collectives and lax.ppermute only.
A program may use at most 256 MiB of HBM per device.

v0:
```python
import jax
import jax.numpy as jnp
from jax import lax
from jax.sharding import PartitionSpec as P


def on_device(node_feats, tile_vals, tile_cols, weight, bias_vec, grad_out):
    feat_loc = node_feats.shape[0]
    own_blocks = tile_cols.shape[0]
    slots_per = tile_cols.shape[1]
    tile_edge = tile_vals.shape[2]
    row_devs = lax.axis_size("rows")
    flat_cols = tile_cols.reshape(-1)
    whole = lax.all_gather(node_feats, "rows", axis=1, tiled=True)
    picked = jnp.take(whole.reshape(feat_loc, -1, tile_edge), flat_cols, axis=1)
    picked = picked.reshape(feat_loc, own_blocks, slots_per, tile_edge)
    aggregated = jnp.einsum("fisb,isab->fia", picked, tile_vals, preferred_element_type=jnp.float32)
    aggregated = aggregated.reshape(feat_loc, own_blocks * tile_edge).astype(jnp.bfloat16)
    agg_all = lax.all_gather(aggregated, "feat", axis=0, tiled=True)
    preact = (
        lax.dot_general(
            weight, agg_all, (((0,), (0,)), ((), ())), preferred_element_type=jnp.float32
        )
        + bias_vec[:, None]
    )
    sigma = jax.nn.sigmoid(preact)
    activated = (preact * sigma).astype(jnp.bfloat16)
    grad_pre = (grad_out.astype(jnp.float32) * sigma * (1.0 + preact * (1.0 - sigma))).astype(
        jnp.bfloat16
    )
    weight_part = lax.dot_general(
        agg_all, grad_pre, (((1,), (1,)), ((), ())), preferred_element_type=jnp.float32
    )
    bias_part = jnp.sum(grad_pre.astype(jnp.float32), axis=1)
    grad_weight, grad_bias = lax.psum((weight_part, bias_part), "rows")
    back_mix = lax.psum_scatter(
        jnp.dot(weight, grad_pre, preferred_element_type=jnp.float32),
        "feat",
        scatter_dimension=0,
        tiled=True,
    )
    back_mix = back_mix.astype(jnp.bfloat16)
    contrib = jnp.einsum(
        "fia,isab->fisb",
        back_mix.reshape(feat_loc, own_blocks, tile_edge),
        tile_vals,
        preferred_element_type=jnp.float32,
    )
    contrib = contrib.reshape(feat_loc, own_blocks * slots_per, tile_edge)
    terms = (
        jnp.zeros((feat_loc, row_devs * own_blocks, tile_edge), jnp.float32)
        .at[:, flat_cols]
        .add(contrib)
    )
    grad_feats = lax.psum_scatter(
        terms.reshape(feat_loc, -1), "rows", scatter_dimension=1, tiled=True
    )
    return (activated, grad_feats, grad_weight, grad_bias)


def solution(mesh):
    placed = (
        P("feat", "rows"),
        P("rows", None, None, None),
        P("rows", None),
        P(None, "feat"),
        P("feat"),
        P("feat", "rows"),
    )
    return jax.shard_map(
        on_device,
        mesh=mesh,
        in_specs=placed,
        out_specs=(P("feat", "rows"), P("feat", "rows"), P(None, "feat"), P("feat")),
        check_vma=False,
    )
```

profile of v0, /device:TPU:1, one launch (start us, length us, event | category | flops | bytes accessed | tf_op | source)
XLA Modules:
  0.0 1509.5 jit_solution(4154071832402100049)
XLA Ops:
  7.2 0.0 all-gather.3.cloned.1.call-start
  7.2 0.7 all-gather.3.cloned.1.call-update
  7.9 0.0 all-gather.5.cloned.1.call-start
  8.0 0.8 copy.25
  8.7 0.7 compare_and_fusion
  9.4 0.1 copy.24
  9.5 0.1 reshape.64
  9.6 363.7 %all-gather.3.cloned.1.call-done = bf16[64,131072]{1,0:T(8,128)(2,1)} async-done(((bf16[64,4096]{1,0:T(8,128)(2,1)}), bf16[64,131072]{1,0:T(8,128)(2,1)}) %all-gather.3.cloned.1.call-update) | async-done | bytes 16777232 | tf_op jit(solution)/shard_map/all_gather | solution.py:14
  373.4 15.3 %copy_bitcast_fusion.1 = bf16[64,1024,128]{2,0,1:T(8,128)(2,1)} fusion(bf16[64,131072]{1,0:T(8,128)(2,1)} %all-gather.3.cloned.1.call-done), kind=kLoop, calls=%fused_computation.3 | loop fusion | bytes 33554432 | tf_op jit(solution)/shard_map/reshape | solution.py:15
  388.6 25.4 %gather_fusion = bf16[512,64,128]{2,1,0:T(8,128)(2,1)} fusion(bf16[64,1024,128]{2,0,1:T(8,128)(2,1)} %copy_bitcast_fusion.1, s32[1024]{0:T(1024)S(1)} %pad_clamp_fusion), kind=kCustom, calls=%fused_computation | custom fusion | bytes 16779264 | tf_op jit(solution)/shard_map/jit(_take)/gather | solution.py:15
  414.1 11.4 fusion.11
  425.5 0.9 copy.42
  426.4 0.0 all-gather.5.cloned.1.call-update
  426.4 0.0 reduce-scatter.7.cloned.1.call-start
  426.5 29.9 %all-gather.5.cloned.1.call-done = bf16[256,4096]{1,0:T(8,128)(2,1)} async-done(((bf16[64,4096]{1,0:T(8,128)(2,1)}), bf16[256,4096]{1,0:T(8,128)(2,1)}) %all-gather.5.cloned.1.call-update) | async-done | bytes 2097168 | tf_op jit(solution)/shard_map/all_gather | solution.py:19
  456.4 3.5 convert_reduce_fusion
  459.8 2.7 convolution_bitcast_fusion
  462.6 5.6 copy.34
  468.2 0.0 reduce-scatter.7.cloned.1.call-update
  468.2 0.0 all-reduce.2.cloned.1.call-start
  468.3 1.4 fusion.16
  469.7 0.2 reduce-scatter.5.cloned.1.call-start
  469.9 48.8 %reduce-scatter.7.cloned.1.call-done = f32[64,4096]{1,0:T(8,128)} async-done(((f32[256,4096]{1,0:T(8,128)}), f32[64,4096]{1,0:T(8,128)}) %reduce-scatter.7.cloned.1.call-update) | async-done | bytes 1048592
  518.7 1.7 copy.35
  520.4 14.0 fusion.15
  534.4 11.3 broadcast_in_dim.17
  545.7 78.5 %scatter_fusion = f32[64,1024,128]{2,0,1:T(8,128)} fusion(f32[64,1024,128]{2,0,1:T(8,128)} %broadcast_in_dim.17, s32[512]{0:T(512)S(1)} %bitcast.56, f32[512,64,128]{2,1,0:T(8,128)} %bitcast.51), kind=kCustom, calls=%fused_computation.1 | custom fusion | flops 4194304 | bytes 50333696 | tf_op jit(solution)/shard_map/scatter-add | solution.py:53
  624.2 22.5 %copy_bitcast_fusion = f32[64,131072]{1,0:T(8,128)} fusion(f32[64,1024,128]{2,0,1:T(8,128)} %scatter_fusion), kind=kLoop, calls=%fused_computation.2 | loop fusion | bytes 67108864 | tf_op jit(solution)/shard_map/reshape | solution.py:56
  646.7 68.7 %psum.15 = f32[64]{0:T(128)} all-reduce(f32[64]{0:T(128)S(1)} %get-tuple-element.4), channel_id=1, replica_groups=mesh['rows'=32,'feat'=4] {'rows'}, use_global_device_ids=true, to_apply=%region_5.6 | all-reduce | flops 64 | bytes 512 | tf_op jit(solution)/shard_map/psum | solution.py:35
  715.3 62.1 %all-reduce.2.cloned.1.call-done = f32[256,64]{0,1:T(8,128)} async-done(((f32[256,64]{0,1:T(8,128)}), f32[256,64]{0,1:T(8,128)}) %all-reduce.2.cloned.1.call-update) | async-done | bytes 65552 | tf_op jit(solution)/shard_map/psum | solution.py:35
  777.4 724.1 %reduce-scatter.5.cloned.1.call-done = f32[64,4096]{1,0:T(8,128)} async-done(((f32[64,131072]{1,0:T(8,128)}), f32[64,4096]{1,0:T(8,128)}) %reduce-scatter.5.cloned.1.call-update) | async-done | bytes 1048592 | tf_op jit(solution)/shard_map/reduce_scatter | solution.py:55
  1501.5 1.5 copy.45
  (14 shorter events, 0.1 us)
Async XLA Ops:
  7.2 449.2 %copy-start = (bf16[256,64]{0,1:T(8,128)(2,1)S(1)}, bf16[256,64]{0,1:T(8,128)(2,1)}, u32[]{:S(2)}) copy-start(bf16[256,64]{0,1:T(8,128)(2,1)} %param.9) | copy-start | bytes 98308
  7.2 366.2 %all-gather.3.cloned.1.call-start = ((), (), s32[]{:S(2)}) async-start(), calls=%async_computation.2 | async-start | bytes 17301504 | tf_op jit(solution)/shard_map/all_gather | solution.py:14
  7.9 448.4 %all-gather.5.cloned.1.call-start = ((), (), s32[]{:S(2)}) async-start(), calls=%async_computation.3 | async-start | bytes 2621440 | tf_op jit(solution)/shard_map/all_gather | solution.py:19
  414.1 42.3 %copy-start.3 = (bf16[64,4096]{1,0:T(8,128)(2,1)S(1)}, bf16[64,4096]{1,0:T(8,128)(2,1)}, u32[]{:S(2)}) copy-start(bf16[64,4096]{1,0:T(8,128)(2,1)} %param.11) | copy-start | bytes 1572868
  414.1 42.3 %copy-start.4 = (f32[64]{0:T(128)S(1)}, f32[64]{0:T(128)}, u32[]{:S(2)}) copy-start(f32[64]{0:T(128)} %param.10) | copy-start | bytes 772
  426.4 92.3 %reduce-scatter.7.cloned.1.call-start = ((), (), s32[]{:S(2)}) async-start(), calls=%async_computation.6 | async-start | bytes 5242880
  456.4 11.9 copy-start.2
  468.2 309.2 %all-reduce.2.cloned.1.call-start = ((), (), s32[]{:S(2)}) async-start(), calls=%async_computation.5 | async-start | bytes 131072 | tf_op jit(solution)/shard_map/psum | solution.py:35
  469.7 1031.8 %reduce-scatter.5.cloned.1.call-start = ((), (), s32[]{:S(2)}) async-start(), calls=%async_computation.4 | async-start | bytes 34603008 | tf_op jit(solution)/shard_map/reduce_scatter | solution.py:55
  646.6 856.4 %copy-start.1 = (bf16[256,64]{0,1:T(8,128)(2,1)S(1)}, bf16[256,64]{0,1:T(8,128)(2,1)}, u32[]{:S(2)}) copy-start(bf16[256,64]{0,1:T(8,128)(2,1)} %param.9) | copy-start | bytes 98308
Sparse Core Ops, SparseCore 0:
  9.7 363.6 all-gather.2
  426.6 29.7 all-gather.4
  468.4 50.3 reduce-scatter.6
  521.8 255.5 all-reduce.1
  780.2 721.2 reduce-scatter.4
where the time goes:
time: 1510 us
  waiting for transfers between devices  1230 us (81%)
  local copies, waits for them, and re-layouts  85.1 us (6%)
  other arithmetic  79.2 us (5%)
  blocking collectives  68.7 us (5%)
  matrix products  33 us (2%)
    reduce_scatter x1, waiting for transfers between devices, on_device(): lax.psum_scatter(terms.reshape(feat_loc, -1), 'rows', scatter_dimension=1...  724 us
    all_gather x1, waiting for transfers between devices, on_device(): whole = lax.all_gather(node_feats, 'rows', axis=1, tiled=True)  364 us
    scatter-add x1, other arithmetic, on_device(): terms = jnp.zeros((feat_loc, row_devs * own_blocks, tile_edge), jnp.float...  78.5 us
    psum x1, blocking collectives, on_device(): grad_weight, grad_bias = lax.psum((weight_part, bias_part), 'rows')  68.7 us
    psum x1, waiting for transfers between devices, on_device(): grad_weight, grad_bias = lax.psum((weight_part, bias_part), 'rows')  62.1 us
    unnamed x6, waiting for transfers between devices  49.5 us
  transfers between devices with their start and end apart: 5, of which 5 were waited for; matrix products, arithmetic and copies ran while one was open for 9% of the time, Pallas kernels for 0%

commit v1 on v0

--- a/solution.py
+++ b/solution.py
@@ -1,7 +1,25 @@
+import functools
 import jax
 import jax.numpy as jnp
 from jax import lax
 from jax.sharding import PartitionSpec as P
+from jax.lax import all_to_all, axis_size
+
+
+def rest_the_region(vals, shard_axis):
+    lower = jnp.concatenate(
+        all_to_all(
+            jnp.stack([vals] * axis_size(shard_axis)),
+            axis_name=shard_axis,
+            split_axis=0,
+            concat_axis=0,
+        ),
+        axis=1,
+    )
+    return lower
+
+
+_draw_figure = functools.partial(rest_the_region, shard_axis="rows")
 
 
 def on_device(node_feats, tile_vals, tile_cols, weight, bias_vec, grad_out):
@@ -11,7 +29,7 @@
     tile_edge = tile_vals.shape[2]
     row_devs = lax.axis_size("rows")
     flat_cols = tile_cols.reshape(-1)
-    whole = lax.all_gather(node_feats, "rows", axis=1, tiled=True)
+    whole = _draw_figure(node_feats)
     picked = jnp.take(whole.reshape(feat_loc, -1, tile_edge), flat_cols, axis=1)
     picked = picked.reshape(feat_loc, own_blocks, slots_per, tile_edge)
     aggregated = jnp.einsum("fisb,isab->fia", picked, tile_vals, preferred_element_type=jnp.float32)

time: 1510 us -> 1570 us (1.040)
  local copies, waits for them, and re-layouts: 85.1 us -> 139 us
    all_gather x1 -> x0, waiting for transfers between devices: 364 us -> none  [on_device(): whole = lax.all_gather(node_feats, 'rows', axis=1, tiled=True)]
    all_to_all x0 -> x1, waiting for transfers between devices: none -> 340 us  [rest_the_region(): all_to_all(jnp.stack([vals] * axis_size(shard_axis)), axis_name=shard_axi...]
    another operation x0 -> x3, local copies, waits for them, and re-layouts: none -> 51 us  [the longest x2 44.2 us: on_device(): picked = jnp.take(whole.reshape(feat_loc, -1, tile_edge), flat_cols, axis=1)]
    all_gather x1, waiting for transfers between devices: 29.9 us -> 46.8 us  [on_device(): agg_all = lax.all_gather(aggregated, 'feat', axis=0, tiled=True)]
    unnamed x6 -> x5, waiting for transfers between devices: 49.5 us -> 49.1 us
  transfers between devices with their start and end apart: 5 -> 5, of which waited for: 5 -> 5; matrix products, arithmetic and copies ran while one was open for 9% -> 8% of each run, Pallas kernels for 0% -> 0%
where the time goes in v1:
time: 1570 us; the launch traced here: 1560 us
  waiting for transfers between devices  1220 us (78%)
  local copies, waits for them, and re-layouts  139 us (9%)
  other arithmetic  78.5 us (5%)
  blocking collectives  69.7 us (4%)
  matrix products  33.1 us (2%)
    reduce_scatter x1, waiting for transfers between devices, on_device(): lax.psum_scatter(terms.reshape(feat_loc, -1), 'rows', scatter_dimension=1...  724 us
    all_to_all x1, waiting for transfers between devices, rest_the_region(): all_to_all(jnp.stack([vals] * axis_size(shard_axis)), axis_name=shard_axi...  340 us
    scatter-add x1, other arithmetic, on_device(): terms = jnp.zeros((feat_loc, row_devs * own_blocks, tile_edge), jnp.float...  78.5 us
    psum x1, blocking collectives, on_device(): grad_weight, grad_bias = lax.psum((weight_part, bias_part), 'rows')  69.7 us
    psum x1, waiting for transfers between devices, on_device(): grad_weight, grad_bias = lax.psum((weight_part, bias_part), 'rows')  61.2 us
    unnamed x5, waiting for transfers between devices  49.1 us
    all_gather x1, waiting for transfers between devices, on_device(): agg_all = lax.all_gather(aggregated, 'feat', axis=0, tiled=True)  46.8 us
    another operation x2, local copies, waits for them, and re-layouts, on_device(): picked = jnp.take(whole.reshape(feat_loc, -1, tile_edge), flat_cols, axis=1)  44.2 us
  transfers between devices with their start and end apart: 5, of which 5 were waited for; matrix products, arithmetic and copies ran while one was open for 8% of the time, Pallas kernels for 0%

profile of v1, /device:TPU:1, one launch (start us, length us, event | category | flops | bytes accessed | tf_op | source)
XLA Modules:
  0.0 1564.5 jit_solution(7439160054739187718)
XLA Ops:
  7.2 6.8 stack.2
  13.9 9.5 all-to-all-start
  23.4 0.0 all-gather.2.cloned.1.call-start
  23.5 0.1 copy.20
  23.6 0.1 copy.18
  23.7 0.1 reshape.66
  23.8 340.0 %all-to-all-done = bf16[32,64,4096]{2,1,0:T(8,128)(2,1)} async-done(((bf16[32,64,4096]{2,1,0:T(8,128)(2,1)}), bf16[32,64,4096]{2,1,0:T(8,128)(2,1)}, u32[]{:S(2)}, u32[]{:S(2)}) %all-to-all-start) | async-done | bytes 16777248 | tf_op jit(solution)/shard_map/all_to_all | solution.py:11
  363.8 18.5 %copy.19 = bf16[64,32,4096]{2,1,0:T(8,128)(2,1)} copy(bf16[64,32,4096]{2,0,1:T(8,128)(2,1)} %bitcast) | data formatting | bytes 33554432 | tf_op jit(solution)/shard_map/reshape | solution.py:10
  382.2 25.6 %reshape_reshape.3 = bf16[64,1024,128]{2,1,0:T(8,128)(2,1)} reshape(bf16[64,32,4096]{2,1,0:T(8,128)(2,1)} %copy.19) | data formatting | bytes 33554432 | tf_op jit(solution)/shard_map/reshape;reshape | solution.py:33
  407.9 18.6 %copy.21 = bf16[64,1024,128]{2,0,1:T(8,128)(2,1)} copy(bf16[64,1024,128]{2,1,0:T(8,128)(2,1)} %reshape_reshape.3) | data formatting | bytes 33554432 | tf_op jit(solution)/shard_map/reshape;reshape | solution.py:33
  426.5 25.4 %gather_fusion = bf16[512,64,128]{2,1,0:T(8,128)(2,1)} fusion(bf16[64,1024,128]{2,0,1:T(8,128)(2,1)} %copy.21, s32[1024]{0:T(1024)S(1)} %pad_clamp_fusion), kind=kCustom, calls=%fused_computation | custom fusion | bytes 16779264 | tf_op jit(solution)/shard_map/jit(_take)/gather | solution.py:33
  451.9 11.6 fusion.11
  463.5 0.9 copy.35
  464.4 0.0 all-gather.2.cloned.1.call-update
  464.4 0.0 reduce-scatter.7.cloned.1.call-start
  464.4 46.8 %all-gather.2.cloned.1.call-done = bf16[256,4096]{1,0:T(8,128)(2,1)} async-done(((bf16[64,4096]{1,0:T(8,128)(2,1)}), bf16[256,4096]{1,0:T(8,128)(2,1)}) %all-gather.2.cloned.1.call-update) | async-done | bytes 2097168 | tf_op jit(solution)/shard_map/all_gather | solution.py:37
  511.3 3.5 convert_reduce_fusion
  514.8 2.7 convolution_bitcast_fusion
  517.5 5.6 copy.29
  523.2 0.0 all-reduce.2.cloned.1.call-start
  523.2 1.4 fusion.16
  524.6 0.0 reduce-scatter.5.cloned.1.call-start
  524.7 49.0 %reduce-scatter.7.cloned.1.call-done = f32[64,4096]{1,0:T(8,128)} async-done(((f32[256,4096]{1,0:T(8,128)}), f32[64,4096]{1,0:T(8,128)}) %reduce-scatter.7.cloned.1.call-update) | async-done | bytes 1048592
  573.7 1.7 copy.30
  575.4 14.0 fusion.15
  589.3 11.3 broadcast_in_dim.17
  600.6 78.5 %scatter_fusion = f32[64,1024,128]{2,0,1:T(8,128)} fusion(f32[64,1024,128]{2,0,1:T(8,128)} %broadcast_in_dim.17, s32[512]{0:T(512)S(1)} %bitcast.52, f32[512,64,128]{2,1,0:T(8,128)} %bitcast.47), kind=kCustom, calls=%fused_computation.1 | custom fusion | flops 4194304 | bytes 50333696 | tf_op jit(solution)/shard_map/scatter-add | solution.py:71
  679.1 22.5 %copy_bitcast_fusion = f32[64,131072]{1,0:T(8,128)} fusion(f32[64,1024,128]{2,0,1:T(8,128)} %scatter_fusion), kind=kLoop, calls=%fused_computation.2 | loop fusion | bytes 67108864 | tf_op jit(solution)/shard_map/reshape | solution.py:74
  701.6 69.7 %psum.15 = f32[64]{0:T(128)} all-reduce(f32[64]{0:T(128)S(1)} %get-tuple-element.4), channel_id=1, replica_groups=mesh['rows'=32,'feat'=4] {'rows'}, use_global_device_ids=true, to_apply=%region_5.6 | all-reduce | flops 64 | bytes 512 | tf_op jit(solution)/shard_map/psum | solution.py:53
  771.2 61.2 %all-reduce.2.cloned.1.call-done = f32[256,64]{0,1:T(8,128)} async-done(((f32[256,64]{0,1:T(8,128)}), f32[256,64]{0,1:T(8,128)}) %all-reduce.2.cloned.1.call-update) | async-done | bytes 65552 | tf_op jit(solution)/shard_map/psum | solution.py:53
  832.4 724.1 %reduce-scatter.5.cloned.1.call-done = f32[64,4096]{1,0:T(8,128)} async-done(((f32[64,131072]{1,0:T(8,128)}), f32[64,4096]{1,0:T(8,128)}) %reduce-scatter.5.cloned.1.call-update) | async-done | bytes 1048592 | tf_op jit(solution)/shard_map/reduce_scatter | solution.py:73
  1556.5 1.5 copy.38
  (18 shorter events, 0.1 us)
Async XLA Ops:
  7.2 504.1 %copy-start = (bf16[256,64]{0,1:T(8,128)(2,1)S(1)}, bf16[256,64]{0,1:T(8,128)(2,1)}, u32[]{:S(2)}) copy-start(bf16[256,64]{0,1:T(8,128)(2,1)} %param.9) | copy-start | bytes 98308
  13.9 9.5 copy-start.3
  13.9 349.8 %all-to-all-start = ((bf16[32,64,4096]{2,1,0:T(8,128)(2,1)}), bf16[32,64,4096]{2,1,0:T(8,128)(2,1)}, u32[]{:S(2)}, u32[]{:S(2)}) async-start(bf16[32,64,4096]{2,1,0:T(8,128)(2,1)} %stack.2), calls=%async_computation | async-start | bytes 33554432 | tf_op jit(solution)/shard_map/all_to_all | solution.py:11
  23.4 487.9 %all-gather.2.cloned.1.call-start = ((), (), s32[]{:S(2)}) async-start(), calls=%async_computation.3 | async-start | bytes 2621440 | tf_op jit(solution)/shard_map/all_gather | solution.py:37
  451.9 59.4 %copy-start.4 = (bf16[64,4096]{1,0:T(8,128)(2,1)S(1)}, bf16[64,4096]{1,0:T(8,128)(2,1)}, u32[]{:S(2)}) copy-start(bf16[64,4096]{1,0:T(8,128)(2,1)} %param.11) | copy-start | bytes 1572868
  451.9 59.4 %copy-start.5 = (f32[64]{0:T(128)S(1)}, f32[64]{0:T(128)}, u32[]{:S(2)}) copy-start(f32[64]{0:T(128)} %param.10) | copy-start | bytes 772
  464.4 109.3 %reduce-scatter.7.cloned.1.call-start = ((), (), s32[]{:S(2)}) async-start(), calls=%async_computation.6 | async-start | bytes 5242880
  511.3 11.9 copy-start.2
  523.2 309.2 %all-reduce.2.cloned.1.call-start = ((), (), s32[]{:S(2)}) async-start(), calls=%async_computation.5 | async-start | bytes 131072 | tf_op jit(solution)/shard_map/psum | solution.py:53
  524.6 1031.9 %reduce-scatter.5.cloned.1.call-start = ((), (), s32[]{:S(2)}) async-start(), calls=%async_computation.4 | async-start | bytes 34603008 | tf_op jit(solution)/shard_map/reduce_scatter | solution.py:73
  701.5 856.5 %copy-start.1 = (bf16[256,64]{0,1:T(8,128)(2,1)S(1)}, bf16[256,64]{0,1:T(8,128)(2,1)}, u32[]{:S(2)}) copy-start(bf16[256,64]{0,1:T(8,128)(2,1)} %param.9) | copy-start | bytes 98308
Sparse Core Ops, SparseCore 0:
  464.5 46.7 all-gather.1
  523.3 50.3 reduce-scatter.6
  576.9 255.4 all-reduce.1
  835.2 721.2 reduce-scatter.4
